TPU v7x, 32 devices: a whole 2x2x4 slice. The times are simulated.
32 devices in a mesh: head: 4 (over y, x), batch: 8 (over z, core).
Axes of the slice: x: 2, y: 2, z: 4, core: 2. Of those that a mesh axis runs over, the one named last changes fastest.
Arguments:
- hidden_in: bfloat16 [8, 256, 4096], P('batch', None, 'head')
- w_query: bfloat16 [4096, 4096], P('batch', 'head'), may hold values from -0.09375 to 0.09375
- w_key: bfloat16 [4096, 4096], P('batch', 'head'), may hold values from -0.09375 to 0.09375
- w_value: bfloat16 [4096, 4096], P('batch', 'head'), may hold values from -0.09375 to 0.09375
- w_beta: bfloat16 [4096, 32], P('batch', 'head'), may hold values from -0.09375 to 0.09375
- w_out: bfloat16 [4096, 4096], P('head', 'batch'), may hold values from -0.125 to 0.125
- mem_pos: int32 [8, 2, 64], P('batch'), may hold values from 0 to 127, as said below
- memory_in: float32 [8, 32, 128, 128], P('batch', 'head'), may hold values from -6 to 6
Outputs:
- hidden_out: bfloat16 [8, 256, 4096], P('batch', None, 'head')
- memory_out: float32 [8, 32, 128, 128], P('batch', 'head')
Inputs may be any that keep to these rules, and one draw needn't show every extreme that they name: `mem_pos`: within each sequence and segment the 64 positions are distinct and ascending.
All inputs are finite; a program needn't handle non-finite values.
Results may differ from a plain program's by a relative error of at most 0.005.
Values may be sent and summed in bfloat16 or wider, within the bound.
No kernel may reach another device: no remote copies, remote signals or barrier semaphores. Data moves between devices by JAX's collectives and lax.ppermute only.
A program may use at most 128 MiB of HBM per device.

v0:
```python
import jax
import jax.numpy as jnp
from jax import lax
from jax.sharding import PartitionSpec as P

SEGS = 2
epsilon = 1e-05


def recur(query, keys, values, beta, state):
    highest = lax.Precision.HIGHEST
    readouts = []
    for segment in range(query.shape[1]):
        readouts.append(
            jnp.einsum("bhij,blhj->blhi", state, query[:, segment], precision=highest).astype(
                jnp.bfloat16
            )
        )
        recalled = jnp.einsum("bhij,bmhj->bmhi", state, keys[:, segment], precision=highest)
        change = beta[:, segment][..., None] * (values[:, segment] - recalled)
        state = state + jnp.einsum("bmhi,bmhj->bhij", change, keys[:, segment], precision=highest)
    return (jnp.stack(readouts, axis=1), state)


def body(hidden_in, w_query, w_key, w_value, w_beta, w_out, mem_pos, memory_in):
    seq_count, row_count, local_width = hidden_in.shape
    seg_rows = row_count // SEGS
    mem_count = mem_pos.shape[2]
    local_heads = w_beta.shape[1]
    local_features = w_query.shape[1]
    head_size = local_features // local_heads
    x_float = hidden_in.astype(jnp.float32)
    whole = lax.all_gather(hidden_in, "head", axis=2, tiled=True)
    whole_float = whole.astype(jnp.float32)
    mean_square = jnp.mean(whole_float * whole_float, axis=2, keepdims=True)
    normed = (whole_float * lax.rsqrt(mean_square + epsilon)).astype(jnp.bfloat16)
    full_width = normed.shape[2]
    offsets = (jnp.arange(SEGS, dtype=jnp.int32) * seg_rows)[None, :, None]
    picked = (mem_pos + offsets).reshape(seq_count, SEGS * mem_count)
    memory_rows = jax.vmap(lambda block, where: jnp.take(block, where, axis=0))(normed, picked)
    memory_rows = memory_rows.reshape(seq_count * SEGS * mem_count, full_width)
    token_rows = normed.reshape(seq_count * row_count, full_width)
    piece_query = lax.all_gather(w_query, "batch", axis=0, tiled=True)
    piece_key = lax.all_gather(w_key, "batch", axis=0, tiled=True)
    piece_value = lax.all_gather(w_value, "batch", axis=0, tiled=True)
    piece_beta = lax.all_gather(w_beta, "batch", axis=0, tiled=True)
    query = jnp.dot(token_rows, piece_query, preferred_element_type=jnp.float32)
    keys = jnp.dot(memory_rows, piece_key, preferred_element_type=jnp.float32)
    values = jnp.dot(memory_rows, piece_value, preferred_element_type=jnp.float32)
    logits = jnp.dot(memory_rows, piece_beta, preferred_element_type=jnp.float32)
    query = (query * head_size ** (-0.5)).reshape(seq_count, SEGS, seg_rows, local_heads, head_size)
    keys = keys.reshape(seq_count, SEGS, mem_count, local_heads, head_size)
    keys = keys * lax.rsqrt(jnp.sum(keys * keys, axis=-1, keepdims=True) + 1e-06)
    values = values.reshape(seq_count, SEGS, mem_count, local_heads, head_size)
    beta = jax.nn.sigmoid(logits).reshape(seq_count, SEGS, mem_count, local_heads)
    readout, state = recur(query, keys, values, beta, memory_in)
    readout = readout.reshape(seq_count * row_count, local_features)
    terms = jnp.dot(
        readout,
        lax.all_gather(w_out, "batch", axis=1, tiled=True),
        preferred_element_type=jnp.float32,
    )
    mixed = lax.psum_scatter(terms, "head", scatter_dimension=1, tiled=True)
    hidden_out = (mixed + x_float.reshape(seq_count * row_count, local_width)).astype(jnp.bfloat16)
    return (hidden_out.reshape(hidden_in.shape), state)


def solution(mesh):
    in_specs = (
        P("batch", None, "head"),
        P("batch", "head"),
        P("batch", "head"),
        P("batch", "head"),
        P("batch", "head"),
        P("head", "batch"),
        P("batch", None, None),
        P("batch", "head", None, None),
    )
    out_specs = (P("batch", None, "head"), P("batch", "head", None, None))
    return jax.shard_map(body, mesh=mesh, in_specs=in_specs, out_specs=out_specs, check_vma=False)
```

profile of v0, /device:TPU:0, one launch (start us, length us, event | category | flops | bytes accessed | tf_op | source)
XLA Modules:
  0.0 445.6 jit_solution(10736198151364103323)
XLA Ops:
  7.2 0.7 all-gather.6.cloned.1.call-update
  7.9 0.7 all-gather.12.cloned.1.call-update
  8.7 0.7 all-gather.10.cloned.1.call-update
  9.4 0.5 all-gather.8.cloned.1.call-update
  10.0 0.5 all-gather.14.cloned.1.call-update
  10.6 0.8 broadcast_add_fusion
  11.5 15.9 %all_gather.20 = bf16[4096,8]{0,1:T(8,128)(2,1)S(1)} all-gather(bf16[512,8]{0,1:T(8,128)(2,1)} %param.12), channel_id=1, replica_groups=mesh['head'=4,'batch'=8] {'batch'}, dimensions={0}, use_global_device_ids=true | all-gather | bytes 73728 | tf_op jit(solution)/shard_map/all_gather | solution.py:46
  27.4 20.3 %all-gather.6.cloned.1.call-done = bf16[1,256,4096]{2,1,0:T(8,128)(2,1)} async-done(((bf16[1,256,1024]{2,1,0:T(8,128)(2,1)}), bf16[1,256,4096]{2,1,0:T(8,128)(2,1)}) %all-gather.6.cloned.1.call-update) | async-done | bytes 2097168 | tf_op jit(solution)/shard_map/all_gather | solution.py:33
  47.8 2.1 fusion
  49.8 2.2 fusion.1
  52.0 3.7 gather_fusion
  55.8 0.4 fusion.22
  56.3 1.2 bitcast_select_fusion
  57.5 73.9 %all-gather.12.cloned.1.call-done = bf16[4096,1024]{1,0:T(8,128)(2,1)} async-done(((bf16[512,1024]{1,0:T(8,128)(2,1)}), bf16[4096,1024]{1,0:T(8,128)(2,1)}) %all-gather.12.cloned.1.call-update) | async-done | bytes 8388624 | tf_op jit(solution)/shard_map/all_gather | solution.py:44
  131.4 4.7 %convolution_bitcast_fusion.2 = f32[16,8,8,128]{3,1,2,0:T(8,128)S(1)} fusion(bf16[4096,1024]{1,0:T(8,128)(2,1)} %all-gather.12.cloned.1.call-done, bf16[128,4096]{1,0:T(8,128)(2,1)S(1)} %gather_fusion, pred[128]{0:T(512)(128)(4,1)S(1)} %compare_and_fusion), kind=kOutput, calls=%fused_computation.11 | convolution fusion | flops 1074266112 | bytes 9961600 | tf_op jit(solution)/shard_map/dot_general | solution.py:48
  136.2 0.2 multiply_reduce_fusion
  136.5 77.1 %all-gather.10.cloned.1.call-done = bf16[4096,1024]{1,0:T(8,128)(2,1)} async-done(((bf16[512,1024]{1,0:T(8,128)(2,1)}), bf16[4096,1024]{1,0:T(8,128)(2,1)}) %all-gather.10.cloned.1.call-update) | async-done | bytes 8388624 | tf_op jit(solution)/shard_map/all_gather | solution.py:45
  213.6 12.1 %copy.27 = bf16[1024,4096]{1,0:T(8,128)(2,1)} copy(bf16[1024,4096]{0,1:T(8,128)(2,1)} %bitcast.131) | data formatting | bytes 16777216 | tf_op jit(solution)/shard_map/dot_general | solution.py:49
  225.7 69.9 %all-gather.8.cloned.1.call-done = bf16[4096,1024]{1,0:T(8,128)(2,1)} async-done(((bf16[512,1024]{1,0:T(8,128)(2,1)}), bf16[4096,1024]{1,0:T(8,128)(2,1)}) %all-gather.8.cloned.1.call-update) | async-done | bytes 8388624 | tf_op jit(solution)/shard_map/all_gather | solution.py:43
  295.6 5.9 %fusion.7 = f32[32,8,8,128]{3,1,2,0:T(8,128)S(1)} fusion(bf16[4096,1024]{1,0:T(8,128)(2,1)} %all-gather.8.cloned.1.call-done, bf16[1,256,4096]{2,1,0:T(8,128)(2,1)S(1)} %fusion.1), kind=kOutput, calls=%fused_computation.8 | convolution fusion | flops 2147745792 | bytes 11534336 | tf_op jit(solution)/shard_map/dot_general | solution.py:47
  301.7 1.2 fusion.12
  303.2 2.9 convolution_bitcast_fusion.3
  306.1 1.1 fusion.17
  307.2 1.0 fusion.10
  308.3 1.2 fusion.13
  309.6 0.3 copy.30
  309.9 67.7 %all-gather.14.cloned.1.call-done = bf16[1024,4096]{1,0:T(8,128)(2,1)} async-done(((bf16[1024,512]{1,0:T(8,128)(2,1)}), bf16[1024,4096]{1,0:T(8,128)(2,1)}) %all-gather.14.cloned.1.call-update) | async-done | bytes 8388624 | tf_op jit(solution)/shard_map/all_gather | solution.py:60
  377.6 7.7 %fusion.25 = f32[256,4096]{1,0:T(8,128)} fusion(bf16[1024,4096]{1,0:T(8,128)(2,1)} %all-gather.14.cloned.1.call-done, bf16[32,8,8,128]{3,2,1,0:T(8,128)(2,1)S(1)} %bitcast.136), kind=kOutput, calls=%fused_computation.36 | convolution fusion | flops 2147483648 | bytes 13107200 | tf_op jit(solution)/shard_map/dot_general | solution.py:58
  385.4 1.1 fusion.19
  386.5 1.8 fusion.11
  388.3 48.3 %reduce-scatter.2.cloned.1.call-done = f32[256,1024]{1,0:T(8,128)} async-done(((f32[256,4096]{1,0:T(8,128)}), f32[256,1024]{1,0:T(8,128)}) %reduce-scatter.2.cloned.1.call-update) | async-done | bytes 1048592 | tf_op jit(solution)/shard_map/reduce_scatter | solution.py:63
  436.6 2.2 fusion.24
  (32 shorter events, 1.3 us)
Async XLA Ops:
  7.2 40.6 %all-gather.6.cloned.1.call-start = ((), (), s32[]{:S(2)}) async-start(), calls=%async_computation.1 | async-start | bytes 2621440 | tf_op jit(solution)/shard_map/all_gather | solution.py:33
  7.9 123.5 %all-gather.12.cloned.1.call-start = ((), (), s32[]{:S(2)}) async-start(), calls=%async_computation.4 | async-start | bytes 9437184 | tf_op jit(solution)/shard_map/all_gather | solution.py:44
  8.6 204.9 %all-gather.10.cloned.1.call-start = ((), (), s32[]{:S(2)}) async-start(), calls=%async_computation.3 | async-start | bytes 9437184 | tf_op jit(solution)/shard_map/all_gather | solution.py:45
  9.4 286.2 %all-gather.8.cloned.1.call-start = ((), (), s32[]{:S(2)}) async-start(), calls=%async_computation.2 | async-start | bytes 9437184 | tf_op jit(solution)/shard_map/all_gather | solution.py:43
  10.0 367.6 %all-gather.14.cloned.1.call-start = ((), (), s32[]{:S(2)}) async-start(), calls=%async_computation.5 | async-start | bytes 9437184 | tf_op jit(solution)/shard_map/all_gather | solution.py:60
  10.5 426.0 %reduce-scatter.2.cloned.1.call-start = ((), (), s32[]{:S(2)}) async-start(), calls=%async_computation.6 | async-start | bytes 5242880 | tf_op jit(solution)/shard_map/reduce_scatter | solution.py:63
  225.7 76.1 %copy-start.1 = (f32[1,8,128,128]{3,2,1,0:T(8,128)S(1)}, f32[1,8,128,128]{3,2,1,0:T(8,128)}, u32[]{:S(2)}) copy-start(f32[1,8,128,128]{3,2,1,0:T(8,128)} %param.15) | copy-start | bytes 1572868
  295.6 7.6 %copy-start = (bf16[1024,4096]{1,0:T(8,128)(2,1)S(1)}, bf16[1024,4096]{1,0:T(8,128)(2,1)}, u32[]{:S(2)}) copy-start(bf16[1024,4096]{1,0:T(8,128)(2,1)} %copy.27) | copy-start | bytes 25165828
  295.6 7.6 %copy-start.2 = (bf16[1,128,1,1,1,1,4096]{6,1,5,4,3,2,0:T(8,128)(2,1)S(1)}, bf16[1,128,1,1,1,1,4096]{6,1,5,4,3,2,0:T(8,128)(2,1)}, u32[]{:S(2)}) copy-start(bf16[1,128,1,1,1,1,4096]{6,1,5,4,3,2,0:T(8,128)(2,1)} %bitcast_select_fusion) | copy-start | bytes 3145732
  377.6 59.0 %copy-start.3 = (bf16[1,256,1024]{2,1,0:T(8,128)(2,1)S(1)}, bf16[1,256,1024]{2,1,0:T(8,128)(2,1)}, u32[]{:S(2)}) copy-start(bf16[1,256,1024]{2,1,0:T(8,128)(2,1)} %param.8) | copy-start | bytes 1572868
Sparse Core Ops, SparseCore 0:
  9.8 37.8 all-gather.5
  49.3 82.0 all-gather.11
  133.0 80.5 all-gather.9
  215.0 80.5 all-gather.7
  297.0 80.5 all-gather.13
  385.5 51.0 reduce-scatter.1
where the time goes:
time: 446 us
  waiting for transfers between devices  360 us (81%)
  matrix products  29.1 us (7%)
  local copies, waits for them, and re-layouts  16.9 us (4%)
  blocking collectives  15.9 us (4%)
  between operations  14.3 us (3%)
  other arithmetic  8.83 us (2%)
    all_gather x1, waiting for transfers between devices, body(): piece_value = lax.all_gather(w_value, 'batch', axis=0, tiled=True)  77.1 us
    all_gather x1, waiting for transfers between devices, body(): piece_key = lax.all_gather(w_key, 'batch', axis=0, tiled=True)  73.9 us
    all_gather x1, waiting for transfers between devices, body(): piece_query = lax.all_gather(w_query, 'batch', axis=0, tiled=True)  69.9 us
    all_gather x1, waiting for transfers between devices, body(): lax.all_gather(w_out, 'batch', axis=1, tiled=True)  67.7 us
    reduce_scatter x1, waiting for transfers between devices, body(): mixed = lax.psum_scatter(terms, 'head', scatter_dimension=1, tiled=True)  48.3 us
    all_gather x1, waiting for transfers between devices, body(): whole = lax.all_gather(hidden_in, 'head', axis=2, tiled=True)  20.3 us
    all_gather x1, blocking collectives, body(): piece_beta = lax.all_gather(w_beta, 'batch', axis=0, tiled=True)  15.9 us
    dot_general x1, local copies, waits for them, and re-layouts, body(): jnp.dot(memory_rows, piece_value, preferred_element_type=jnp.float32)  12.1 us
  transfers between devices with their start and end apart: 6, of which 6 were waited for; matrix products, arithmetic and copies ran while one was open for 10% of the time, Pallas kernels for 0%

commit v1 on v0

--- a/solution.py
+++ b/solution.py
@@ -41,7 +41,21 @@
     memory_rows = memory_rows.reshape(seq_count * SEGS * mem_count, full_width)
     token_rows = normed.reshape(seq_count * row_count, full_width)
     piece_query = lax.all_gather(w_query, "batch", axis=0, tiled=True)
-    piece_key = lax.all_gather(w_key, "batch", axis=0, tiled=True)
+
+    def arrays_feed(incoming_x):
+        along_axis = "batch"
+        state_next = jax.lax.axis_size(along_axis)
+        v_now, z_new, clean = (state_next, jax.lax.axis_index(along_axis), incoming_x.shape[0])
+        y1, seen_now = (incoming_x, 1)
+        while seen_now < v_now:
+            queue = []
+            for at in range(v_now):
+                queue.append((at, (at - seen_now) % v_now))
+            y1 = jnp.concatenate([y1, jax.lax.ppermute(y1, along_axis, queue)], axis=0)
+            seen_now = 2 * seen_now
+        return jnp.roll(y1, z_new * clean, axis=0)
+
+    piece_key = arrays_feed(w_key)
     piece_value = lax.all_gather(w_value, "batch", axis=0, tiled=True)
     piece_beta = lax.all_gather(w_beta, "batch", axis=0, tiled=True)
     query = jnp.dot(token_rows, piece_query, preferred_element_type=jnp.float32)

time: 446 us -> 566 us (1.27)
  blocking collectives: 15.9 us -> 321 us
  waiting for transfers between devices: 360 us -> 145 us
  local copies, waits for them, and re-layouts: 16.9 us -> 35.2 us
    all_gather x1, blocking collectives: 15.9 us -> 321 us  [body(): piece_beta = lax.all_gather(w_beta, 'batch', axis=0, tiled=True)]
    ppermute x0 -> x3, waiting for transfers between devices: none -> 94 us  [arrays_feed(): y1 = jnp.concatenate([y1, jax.lax.ppermute(y1, along_axis, queue)], axis=0)]
    all_gather x1, waiting for transfers between devices: 77.1 us -> 0.02 us  [body(): piece_value = lax.all_gather(w_value, 'batch', axis=0, tiled=True)]
    all_gather x1 -> x0, waiting for transfers between devices: 73.9 us -> none  [body(): piece_key = lax.all_gather(w_key, 'batch', axis=0, tiled=True)]
    all_gather x1, waiting for transfers between devices: 69.9 us -> 0.01 us  [body(): piece_query = lax.all_gather(w_query, 'batch', axis=0, tiled=True)]
    all_gather x1, waiting for transfers between devices: 67.7 us -> 0.02 us  [body(): lax.all_gather(w_out, 'batch', axis=1, tiled=True)]
    all_gather x1, waiting for transfers between devices: 20.3 us -> 0.01 us  [body(): whole = lax.all_gather(hidden_in, 'head', axis=2, tiled=True)]
    unnamed x10 -> x37, local copies, waits for them, and re-layouts: 0.31 us -> 13.5 us
  transfers between devices with their start and end apart: 6 -> 8, of which waited for: 6 -> 3; matrix products, arithmetic and copies ran while one was open for 10% -> 12% of each run, Pallas kernels for 0% -> 0%
where the time goes in v1:
time: 566 us; the launch traced here: 565 us
  blocking collectives  321 us (57%)
  waiting for transfers between devices  145 us (26%)
  local copies, waits for them, and re-layouts  35.2 us (6%)
  matrix products  31.4 us (6%)
  between operations  14 us (2%)
  other arithmetic  13.9 us (2%)
    all_gather x1, blocking collectives, body(): piece_beta = lax.all_gather(w_beta, 'batch', axis=0, tiled=True)  321 us
    ppermute x3, waiting for transfers between devices, arrays_feed(): y1 = jnp.concatenate([y1, jax.lax.ppermute(y1, along_axis, queue)], axis=0)  94 us
    reduce_scatter x1, waiting for transfers between devices, body(): mixed = lax.psum_scatter(terms, 'head', scatter_dimension=1, tiled=True)  48 us
    unnamed x37, local copies, waits for them, and re-layouts  13.5 us
    dot_general x1, local copies, waits for them, and re-layouts, body(): jnp.dot(memory_rows, piece_value, preferred_element_type=jnp.float32)  11.5 us
  transfers between devices with their start and end apart: 8, of which 3 were waited for; matrix products, arithmetic and copies ran while one was open for 12% of the time, Pallas kernels for 0%

profile of v1, /device:TPU:0, one launch (start us, length us, event | category | flops | bytes accessed | tf_op | source)
XLA Modules:
  0.0 565.0 jit_solution(6564479289817047539)
XLA Ops:
  10.0 4.6 collective-permute-start
  14.6 12.6 %collective-permute-done = bf16[512,1024]{1,0:T(8,128)(2,1)S(1)} collective-permute-done((bf16[512,1024]{1,0:T(8,128)(2,1)}, bf16[512,1024]{1,0:T(8,128)(2,1)S(1)}, u32[]{:S(2)}, u32[]{:S(2)}) %collective-permute-start) | collective-permute-done | bytes 1048608 | tf_op jit(solution)/shard_map/ppermute | solution.py:54
  27.2 1.9 pad_maximum_fusion.1
  29.7 81.4 %collective-permute-done.1 = bf16[1024,1024]{1,0:T(8,128)(2,1)S(1)} collective-permute-done((bf16[1024,1024]{1,0:T(8,128)(2,1)S(1)}, bf16[1024,1024]{1,0:T(8,128)(2,1)S(1)}, u32[]{:S(2)}, u32[]{:S(2)}) %collective-permute-start.1) | collective-permute-done | bytes 2097184 | tf_op jit(solution)/shard_map/ppermute | solution.py:54
  111.1 2.5 pad_maximum_fusion
  113.8 320.6 %all_gather.17 = bf16[4096,8]{0,1:T(8,128)(2,1)S(1)} all-gather(bf16[512,8]{0,1:T(8,128)(2,1)S(1)} %copy-done.12), channel_id=1, replica_groups=mesh['head'=4,'batch'=8] {'batch'}, dimensions={0}, use_global_device_ids=true | all-gather | bytes 73728 | tf_op jit(solution)/shard_map/all_gather | solution.py:60
  434.4 1.1 constant_dynamic-update-slice_fusion.7
  435.5 2.3 constant_dynamic-update-slice_fusion.6
  437.8 1.5 constant_dynamic-update-slice_fusion.5
  439.3 2.1 fusion.2
  441.4 2.2 fusion.3
  443.6 4.8 gather_fusion
  448.4 1.7 fusion.27
  450.1 2.5 bitcast_select_fusion
  452.7 4.6 constant_dynamic-update-slice_fusion.4
  457.3 1.1 constant_dynamic-update-slice_fusion.3
  458.5 1.1 constant_dynamic-update-slice_fusion.2
  459.5 1.5 constant_dynamic-update-slice_fusion.1
  461.0 4.6 constant_dynamic-update-slice_fusion
  465.6 4.7 fusion.12
  471.0 11.5 %copy.27 = bf16[1024,4096]{1,0:T(8,128)(2,1)} copy(bf16[1024,4096]{0,1:T(8,128)(2,1)} %bitcast.130) | data formatting | bytes 16777216 | tf_op jit(solution)/shard_map/dot_general | solution.py:63
  482.5 5.9 %fusion.9 = f32[32,8,8,128]{3,1,2,0:T(8,128)S(1)} fusion(bf16[4096,1024]{1,0:T(8,128)(2,1)} %all-gather.7.cloned.1.call-done, bf16[1,256,4096]{2,1,0:T(8,128)(2,1)S(1)} %fusion.3), kind=kOutput, calls=%fused_computation.12 | convolution fusion | flops 2147745792 | bytes 11534336 | tf_op jit(solution)/shard_map/dot_general | solution.py:61
  488.7 1.2 fusion.17
  489.9 2.9 convolution_bitcast_fusion.2
  492.8 1.1 fusion.22
  494.0 2.0 fusion.15
  495.9 1.3 fusion.18
  497.6 7.7 %fusion.30 = f32[256,4096]{1,0:T(8,128)} fusion(bf16[1024,4096]{1,0:T(8,128)(2,1)} %all-gather.11.cloned.1.call-done, bf16[32,8,8,128]{3,2,1,0:T(8,128)(2,1)S(1)} %bitcast.135), kind=kOutput, calls=%fused_computation.40 | convolution fusion | flops 2147483648 | bytes 13107200 | tf_op jit(solution)/shard_map/dot_general | solution.py:72
  505.4 1.1 fusion.24
  506.6 1.8 fusion.16
  508.4 48.0 %reduce-scatter.2.cloned.1.call-done = f32[256,1024]{1,0:T(8,128)} async-done(((f32[256,4096]{1,0:T(8,128)}), f32[256,1024]{1,0:T(8,128)}) %reduce-scatter.2.cloned.1.call-update) | async-done | bytes 1048592 | tf_op jit(solution)/shard_map/reduce_scatter | solution.py:77
  556.3 2.2 fusion.29
  (65 shorter events, 5.2 us)
Async XLA Ops:
  7.2 104.0 %copy-start.3 = (bf16[512,1024]{1,0:T(8,128)(2,1)S(1)}, bf16[512,1024]{1,0:T(8,128)(2,1)}, u32[]{:S(2)}) copy-start(bf16[512,1024]{1,0:T(8,128)(2,1)} %param.10) | copy-start | bytes 3145732
  7.2 106.4 %copy-start.13 = (s32[1,2,64]{2,1,0:T(2,128)S(1)}, s32[1,2,64]{2,1,0:T(2,128)}, u32[]{:S(2)}) copy-start(s32[1,2,64]{2,1,0:T(2,128)} %param.14) | copy-start | bytes 1540
  7.2 106.6 %copy-start.12 = (bf16[512,8]{0,1:T(8,128)(2,1)S(1)}, bf16[512,8]{0,1:T(8,128)(2,1)}, u32[]{:S(2)}) copy-start(bf16[512,8]{0,1:T(8,128)(2,1)} %param.12) | copy-start | bytes 24580
  7.2 432.1 %all-gather.5.cloned.1.call-start = ((), (), s32[]{:S(2)}) async-start(), calls=%async_computation.1 | async-start | bytes 2621440 | tf_op jit(solution)/shard_map/all_gather | solution.py:33
  7.9 463.0 %all-gather.9.cloned.1.call-start = ((), (), s32[]{:S(2)}) async-start(), calls=%async_computation.3 | async-start | bytes 9437184 | tf_op jit(solution)/shard_map/all_gather | solution.py:59
  8.7 473.8 %all-gather.7.cloned.1.call-start = ((), (), s32[]{:S(2)}) async-start(), calls=%async_computation.2 | async-start | bytes 9437184 | tf_op jit(solution)/shard_map/all_gather | solution.py:43
  9.4 488.2 %all-gather.11.cloned.1.call-start = ((), (), s32[]{:S(2)}) async-start(), calls=%async_computation.4 | async-start | bytes 9437184 | tf_op jit(solution)/shard_map/all_gather | solution.py:74
  10.0 546.3 %reduce-scatter.2.cloned.1.call-start = ((), (), s32[]{:S(2)}) async-start(), calls=%async_computation.5 | async-start | bytes 5242880 | tf_op jit(solution)/shard_map/reduce_scatter | solution.py:77
  10.0 17.2 %collective-permute-start = (bf16[512,1024]{1,0:T(8,128)(2,1)}, bf16[512,1024]{1,0:T(8,128)(2,1)S(1)}, u32[]{:S(2)}, u32[]{:S(2)}) collective-permute-start(bf16[512,1024]{1,0:T(8,128)(2,1)} %param.10), channel_id=1, source_target_pairs={{0,7},{1,0},{2,1},{3,2},{4,3},{5,4},{6,5},{7,6},{8,15},{9,8},{10,9... | collective-permute-start | bytes 3145736 | tf_op jit(solution)/shard_map/ppermute | solution.py:54
  27.2 83.9 %copy-start.4 = (bf16[512,1024]{1,0:T(8,128)(2,1)}, bf16[512,1024]{1,0:T(8,128)(2,1)S(1)}, u32[]{:S(2)}) copy-start(bf16[512,1024]{1,0:T(8,128)(2,1)S(1)} %collective-permute-done) | copy-start | bytes 3145732
  29.1 82.0 %collective-permute-start.1 = (bf16[1024,1024]{1,0:T(8,128)(2,1)S(1)}, bf16[1024,1024]{1,0:T(8,128)(2,1)S(1)}, u32[]{:S(2)}, u32[]{:S(2)}) collective-permute-start(bf16[1024,1024]{1,0:T(8,128)(2,1)S(1)} %pad_maximum_fusion.1), channel_id=1, source_target_pairs={{0,6},{1,7},{2,0},{3,1},{4,2},{5,3},{6,4},{7,5},{8,14},{9,15},{10,... | collective-permute-start | bytes 6291464 | tf_op jit(solution)/shard_map/ppermute | solution.py:54
  111.1 328.2 %copy-start.1 = (bf16[1024,1024]{1,0:T(8,128)(2,1)}, bf16[1024,1024]{1,0:T(8,128)(2,1)S(1)}, u32[]{:S(2)}) copy-start(bf16[1024,1024]{1,0:T(8,128)(2,1)S(1)} %collective-permute-done.1) | copy-start | bytes 6291460
  113.6 339.1 %collective-permute-start.2 = (bf16[2048,1024]{1,0:T(8,128)(2,1)}, bf16[2048,1024]{1,0:T(8,128)(2,1)}, u32[]{:S(2)}, u32[]{:S(2)}) collective-permute-start(bf16[2048,1024]{1,0:T(8,128)(2,1)} %pad_maximum_fusion), channel_id=1, source_target_pairs={{0,4},{1,5},{2,6},{3,7},{4,0},{5,1},{6,2},{7,3},{8,12},{9,13},{10,... | collective-permute-start | bytes 12582920 | tf_op jit(solution)/shard_map/ppermute | solution.py:54
  450.1 8.4 %copy-start.5 = (bf16[512,1024]{1,0:T(8,128)(2,1)S(1)}, bf16[512,1024]{1,0:T(8,128)(2,1)}, u32[]{:S(2)}) copy-start(bf16[512,1024]{1,0:T(8,128)(2,1)} %copy-done.4) | copy-start | bytes 3145732
  450.1 9.4 %copy-start.2 = (bf16[1024,1024]{1,0:T(8,128)(2,1)S(1)}, bf16[1024,1024]{1,0:T(8,128)(2,1)}, u32[]{:S(2)}) copy-start(bf16[1024,1024]{1,0:T(8,128)(2,1)} %copy-done.1) | copy-start | bytes 6291460
  457.3 8.3 %copy-start.6 = (bf16[128,4096]{1,0:T(8,128)(2,1)S(1)}, bf16[128,4096]{1,0:T(8,128)(2,1)}, u32[]{:S(2)}) copy-start(bf16[128,4096]{1,0:T(8,128)(2,1)} %gather_fusion) | copy-start | bytes 3145732
  470.9 21.9 %copy-start.8 = (f32[1,2,64,8,128]{4,2,3,1,0:T(8,128)}, f32[1,2,64,8,128]{4,2,3,1,0:T(8,128)S(1)}, u32[]{:S(2)}) copy-start(f32[1,2,64,8,128]{4,2,3,1,0:T(8,128)S(1)} %copy_multiply_fusion) | copy-start | bytes 1572868
  482.5 6.2 %copy-start.7 = (f32[1,8,128,128]{3,2,1,0:T(8,128)S(1)}, f32[1,8,128,128]{3,2,1,0:T(8,128)}, u32[]{:S(2)}) copy-start(f32[1,8,128,128]{3,2,1,0:T(8,128)} %param.15) | copy-start | bytes 1572868
  482.5 7.4 %copy-start = (bf16[1024,4096]{1,0:T(8,128)(2,1)S(1)}, bf16[1024,4096]{1,0:T(8,128)(2,1)}, u32[]{:S(2)}) copy-start(bf16[1024,4096]{1,0:T(8,128)(2,1)} %copy.27) | copy-start | bytes 25165828
  482.5 7.4 %copy-start.10 = (bf16[1,128,1,1,1,1,4096]{6,1,5,4,3,2,0:T(8,128)(2,1)S(1)}, bf16[1,128,1,1,1,1,4096]{6,1,5,4,3,2,0:T(8,128)(2,1)}, u32[]{:S(2)}) copy-start(bf16[1,128,1,1,1,1,4096]{6,1,5,4,3,2,0:T(8,128)(2,1)} %bitcast_select_fusion) | copy-start | bytes 3145732
  497.6 7.8 %copy-start.9 = (f32[1,2,64,8,128]{4,2,3,1,0:T(8,128)S(1)}, f32[1,2,64,8,128]{4,2,3,1,0:T(8,128)}, u32[]{:S(2)}) copy-start(f32[1,2,64,8,128]{4,2,3,1,0:T(8,128)} %copy-done.8) | copy-start | bytes 1572868
  497.6 58.7 %copy-start.11 = (bf16[1,256,1024]{2,1,0:T(8,128)(2,1)S(1)}, bf16[1,256,1024]{2,1,0:T(8,128)(2,1)}, u32[]{:S(2)}) copy-start(bf16[1,256,1024]{2,1,0:T(8,128)(2,1)} %param.8) | copy-start | bytes 1572868
Sparse Core Ops, SparseCore 0:
  9.8 37.8 all-gather.4
  49.4 202.2 all-gather.8
  253.3 119.5 all-gather.6
  374.4 86.4 all-gather.10
  505.5 50.7 reduce-scatter.1
